TPU v7x, 256 devices: a whole 4x4x8 slice. The times are simulated.
256 devices in a mesh: band: 8 (over y_hi, x), item: 32 (over y_lo, z, core).
Axes of the slice: x: 4, y: 4 (y_hi: 2, y_lo: 2; y = y_hi * 2 + y_lo), z: 8, core: 2. Of those that a mesh axis runs over, the one named last changes fastest.
Arguments:
- ratings: bfloat16 [49152, 16384], P('band', 'item'), may hold values from -6 to 6
- rating_mask: int32 [384, 16384], P('band', 'item'), may hold values 0 or 1
- attributes: bfloat16 [24576, 16384], P('band', 'item'), may hold values from -6 to 6
- attribute_mask: int32 [192, 16384], P('band', 'item'), may hold values 0 or 1
- user_factors: bfloat16 [49152, 256], P('band', 'item'), as said below
- tag_factors: bfloat16 [24576, 256], P('band', 'item'), as said below
Outputs:
- item_factors: float32 [16384, 256], P('item')
Inputs may be any that keep to these rules, and one draw needn't show every extreme that they name: `user_factors`: user factors of order one over the square root of 49152. `tag_factors`: tag factors of order one over the square root of 24576.
All inputs are finite; a program needn't handle non-finite values. No bound on the sum of `rating_mask` or of `attribute_mask` on one device may be relied on, other than what follows from the above.
Results may differ from a plain program's by a relative error of at most 0.0003.
Values may be sent and summed in bfloat16 or wider, within the bound.
No kernel may reach another device: no remote copies, remote signals or barrier semaphores. Data moves between devices by JAX's collectives and lax.ppermute only.
A program may use at most 64 MiB of HBM per device.

v0:
```python
import jax
import jax.numpy as jnp
from jax import lax
from jax.sharding import PartitionSpec as P

LAMBDA = 0.5
REG = 0.1


def apply_mask(values, mask):
    rows, cols = values.shape
    blocks = mask.shape[0]
    shaped = values.reshape(blocks, rows // blocks, cols) * mask.astype(values.dtype)[:, None, :]
    return shaped.reshape(rows, cols)


def inner(left, right):
    return lax.dot_general(
        left, right, (((0,), (0,)), ((), ())), preferred_element_type=jnp.float32
    )


def solve_rows(factor, rhs):
    half = lax.linalg.triangular_solve(factor, rhs, left_side=False, lower=True, transpose_a=True)
    return lax.linalg.triangular_solve(factor, half, left_side=False, lower=True, transpose_a=False)


def band_gram(partial_gram):
    return lax.psum(partial_gram, "band")


def finish_gram(summed_gram, rank):
    return jnp.linalg.cholesky(summed_gram + REG * jnp.eye(rank, dtype=jnp.float32))


def body(ratings, rating_mask, attributes, attribute_mask, user_factors, tag_factors):
    users = lax.all_gather(user_factors, "item", axis=1, tiled=True)
    tags = lax.all_gather(tag_factors, "item", axis=1, tiled=True)
    rank = users.shape[1]
    partial_gram = inner(users, users) + LAMBDA * inner(tags, tags)
    masked_ratings = apply_mask(ratings, rating_mask)
    masked_attributes = apply_mask(attributes, attribute_mask)
    local_rhs = inner(masked_ratings, users) + LAMBDA * inner(masked_attributes, tags)
    summed_gram = band_gram(partial_gram)
    summed_rhs = lax.psum(local_rhs, "band")
    factor = finish_gram(summed_gram, rank)
    return solve_rows(factor, summed_rhs)


def solution(mesh):
    in_specs = (
        P("band", "item"),
        P("band", "item"),
        P("band", "item"),
        P("band", "item"),
        P("band", "item"),
        P("band", "item"),
    )
    out_specs = P("item", None)
    return jax.shard_map(body, mesh=mesh, in_specs=in_specs, out_specs=out_specs, check_vma=False)
```

profile of v0, /device:TPU:32, one launch (start us, length us, event | category | flops | bytes accessed | tf_op | source)
XLA Modules:
  0.0 317.1 jit_solution(6339761031712931756)
XLA Ops:
  6.5 0.7 all-gather.5.cloned.1.call-update
  7.3 0.7 all-gather.3.cloned.1.call-update
  8.1 0.8 convert_element_type.8
  8.9 0.9 convert_element_type.7
  9.8 2.3 bitcast_multiply_fusion.1
  12.0 1.5 copy-done
  13.5 3.1 bitcast_multiply_fusion
  16.6 58.8 %all-gather.5.cloned.1.call-done = bf16[3072,256]{0,1:T(8,128)(2,1)} async-done(((bf16[3072,8]{0,1:T(8,128)(2,1)}), bf16[3072,256]{0,1:T(8,128)(2,1)}) %all-gather.5.cloned.1.call-update) | async-done | bytes 1572880 | tf_op jit(solution)/shard_map/all_gather | solution.py:38
  75.4 3.2 %convolution_multiply_fusion = f32[512,256]{1,0:T(8,128)} fusion(bf16[3072,512]{1,0:T(8,128)(2,1)S(1)} %bitcast_multiply_fusion.1, bf16[3072,256]{0,1:T(8,128)(2,1)} %all-gather.5.cloned.1.call-done), kind=kOutput, calls=%fused_computation.4 | convolution fusion | flops 805437440 | bytes 5242880 | tf_op jit(solution)/shard_map/dot_general | solution.py:18
  78.6 64.3 %all-gather.3.cloned.1.call-done = bf16[6144,256]{0,1:T(8,128)(2,1)} async-done(((bf16[6144,8]{0,1:T(8,128)(2,1)}), bf16[6144,256]{0,1:T(8,128)(2,1)}) %all-gather.3.cloned.1.call-update) | async-done | bytes 3145744 | tf_op jit(solution)/shard_map/all_gather | solution.py:37
  142.9 4.0 %fusion.13 = f32[256,256]{1,0:T(8,128)S(1)} fusion(bf16[6144,256]{0,1:T(8,128)(2,1)} %all-gather.3.cloned.1.call-done), kind=kOutput, calls=%fused_computation.41 | convolution fusion | flops 805306368 | bytes 3407872 | tf_op jit(solution)/shard_map/dot_general | solution.py:18
  146.9 1.3 fusion
  148.2 4.5 %convolution_add_fusion = f32[512,256]{1,0:T(8,128)} fusion(f32[512,256]{1,0:T(8,128)S(1)} %copy-done.4, bf16[6144,512]{1,0:T(8,128)(2,1)S(1)} %copy-done.1, bf16[6144,256]{0,1:T(8,128)(2,1)} %all-gather.3.cloned.1.call-done), kind=kOutput, calls=%fused_computation.5 | convolution fusion | flops 1610743808 | bytes 10485760 | tf_op jit(solution)/shard_map/dot_general | solution.py:18
  152.8 92.3 %all-reduce.4.cloned.1.call-done = (f32[512,256]{1,0:T(8,128)}, f32[256,256]{1,0:T(8,128)}) async-done(((f32[512,256]{1,0:T(8,128)}, f32[256,256]{1,0:T(8,128)}), (f32[512,256]{1,0:T(8,128)}, f32[256,256]{1,0:T(8,128)})) %all-reduce.4.cloned.1.call-update) | async-done | bytes 786448 | tf_op jit(solution)/shard_map/psum | solution.py:45
  245.1 1.0 select_add_fusion
  246.3 1.0 fusion.3
  247.3 11.7 %cholesky.49 = f32[128,128]{1,0:T(8,128)S(1)} custom-call(f32[128,128]{1,0:T(8,128)S(1)} %cholesky.115), custom_call_target="Cholesky" | custom-call | tf_op jit(solution)/shard_map/jit(cholesky)/cholesky | solution.py:33
  259.1 9.8 %custom-call.16 = f32[1,128,128]{1,2,0:T(8,128)S(1)} custom-call(f32[1,128,128]{2,1,0:T(8,128)S(1)} %get-tuple-element.28), custom_call_target="InvertDiagBlocksLowerTriangular" | custom-call | tf_op jit(solution)/shard_map/jit(cholesky)/cholesky | solution.py:33
  269.4 11.9 %cholesky.103 = f32[128,128]{1,0:T(8,128)S(1)} custom-call(f32[128,128]{1,0:T(8,128)S(1)} %convolution_subtract_fusion.2), custom_call_target="Cholesky" | custom-call | tf_op jit(solution)/shard_map/jit(cholesky)/cholesky | solution.py:33
  281.3 0.7 compare_reduce_fusion
  283.3 3.9 %while.1 = (s32[]{:T(128)}, f32[256,256]{1,0:T(8,128)S(1)}, s32[2,2]{1,0:T(2,128)S(1)}, f32[2,128,128]{2,1,0:T(8,128)S(1)}, s32[]{:T(128)}) while((s32[]{:T(128)}, f32[256,256]{1,0:T(8,128)S(1)}, s32[2,2]{1,0:T(2,128)S(1)}, f32[2,128,128]{2,1,0:T(8,128)S(1)}, s32[]{:T(128)}) %tuple.23), condition=%wide.while_cond, body=%wide.while_body.sunk | while | flops 2 | bytes 131189 | solution.py:24
  283.4 0.6 fusion.30
  283.9 1.4 bitcast_dynamic-update-slice_fusion.2
  285.3 0.6 fusion.30
  285.9 1.4 bitcast_dynamic-update-slice_fusion.2
  287.3 19.7 %custom-call.17 = f32[2,128,128]{1,2,0:T(8,128)S(1)} custom-call(f32[2,128,128]{2,1,0:T(8,128)S(1)} %get-tuple-element.12), custom_call_target="InvertDiagBlocksLowerTriangular" | custom-call | tf_op jit(solution)/shard_map/triangular_solve | solution.py:24
  307.4 0.4 convolution_subtract_fusion.1
  307.7 0.4 fusion.9
  308.1 0.4 fusion.8
  308.5 0.6 convolution_subtract_fusion
  309.1 0.4 fusion.7
  309.6 1.0 copy.8
  (28 shorter events, 1.3 us)
Async XLA Ops:
  6.5 68.9 %all-gather.5.cloned.1.call-start = ((), (), s32[]{:S(2)}) async-start(), calls=%async_computation.1 | async-start | bytes 1622016 | tf_op jit(solution)/shard_map/all_gather | solution.py:38
  7.3 135.6 %all-gather.3.cloned.1.call-start = ((), (), s32[]{:S(2)}) async-start(), calls=%async_computation | async-start | bytes 3244032 | tf_op jit(solution)/shard_map/all_gather | solution.py:37
  8.0 237.1 %all-reduce.4.cloned.1.call-start = ((), (), s32[]{:S(2)}) async-start(), calls=%async_computation.2 | async-start | bytes 1572864 | tf_op jit(solution)/shard_map/psum | solution.py:45
  9.8 3.7 %copy-start = (bf16[6144,512]{1,0:T(8,128)(2,1)S(1)}, bf16[6144,512]{1,0:T(8,128)(2,1)}, u32[]{:S(2)}) copy-start(bf16[6144,512]{1,0:T(8,128)(2,1)} %param.6) | copy-start | bytes 18874372
  78.6 68.3 %copy-start.2 = (bf16[3072,256]{0,1:T(8,128)(2,1)S(1)}, bf16[3072,256]{0,1:T(8,128)(2,1)}, u32[]{:S(2)}) copy-start(bf16[3072,256]{0,1:T(8,128)(2,1)} %all-gather.5.cloned.1.call-done) | copy-start | bytes 4718596
  142.9 5.3 %copy-start.1 = (bf16[6144,512]{1,0:T(8,128)(2,1)S(1)}, bf16[6144,512]{1,0:T(8,128)(2,1)}, u32[]{:S(2)}) copy-start(bf16[6144,512]{1,0:T(8,128)(2,1)} %bitcast_multiply_fusion) | copy-start | bytes 18874372
  146.9 1.3 copy-start.4
  245.1 61.8 %copy-start.3 = (f32[512,256]{1,0:T(8,128)S(1)}, f32[512,256]{1,0:T(8,128)}, u32[]{:S(2)}) copy-start(f32[512,256]{1,0:T(8,128)} %get-tuple-element.21) | copy-start | bytes 1572868
Sparse Core Ops, SparseCore 0:
  9.2 66.1 all-gather.4
  77.3 65.5 all-gather.2
  152.9 92.1 all-reduce.3
where the time goes:
time: 317 us
  waiting for transfers between devices  217 us (68%)
  other arithmetic  63 us (20%)
  matrix products  16 us (5%)
  between operations  14.6 us (5%)
  local copies, waits for them, and re-layouts  6.6 us (2%)
    psum x1, waiting for transfers between devices, body(): summed_rhs = lax.psum(local_rhs, 'band')  92.3 us
    all_gather x1, waiting for transfers between devices, body(): users = lax.all_gather(user_factors, 'item', axis=1, tiled=True)  64.3 us
    all_gather x1, waiting for transfers between devices, body(): tags = lax.all_gather(tag_factors, 'item', axis=1, tiled=True)  58.8 us
    another operation x6, other arithmetic, finish_gram(): jnp.linalg.cholesky(summed_gram + REG * jnp.eye(rank, dtype=jnp.float32))  34.1 us
    another operation x3, other arithmetic, solve_rows(): lax.linalg.triangular_solve(factor, rhs, left_side=False, lower=True, tra...  19.7 us
    dot_general x4, matrix products, inner(): lax.dot_general(left, right, (((0,), (0,)), ((), ())), preferred_element_...  13 us
  transfers between devices with their start and end apart: 3, of which 3 were waited for; matrix products, arithmetic and copies ran while one was open for 3% of the time, Pallas kernels for 0%

commit v1 on v0

--- a/solution.py
+++ b/solution.py
@@ -34,7 +34,8 @@
 
 
 def body(ratings, rating_mask, attributes, attribute_mask, user_factors, tag_factors):
-    users = lax.all_gather(user_factors, "item", axis=1, tiled=True)
+    sent = jnp.stack([user_factors] * lax.axis_size("item"))
+    users = jnp.concatenate(lax.all_to_all(sent, "item", 0, 0), axis=1)
     tags = lax.all_gather(tag_factors, "item", axis=1, tiled=True)
     rank = users.shape[1]
     partial_gram = inner(users, users) + LAMBDA * inner(tags, tags)

time: 317 us -> 279 us (0.88)
  waiting for transfers between devices: 217 us -> 166 us
  starting transfers between devices: 0.08 us -> 10.1 us
  local copies, waits for them, and re-layouts: 6.6 us -> 10.1 us
    all_gather x1 -> x0, waiting for transfers between devices: 64.3 us -> none  [body(): users = lax.all_gather(user_factors, 'item', axis=1, tiled=True)]
    all_gather x1, waiting for transfers between devices: 58.8 us -> 72.7 us  [body(): tags = lax.all_gather(tag_factors, 'item', axis=1, tiled=True)]
    all_to_all x0 -> x1, starting transfers between devices: none -> 10.1 us  [body(): users = jnp.concatenate(lax.all_to_all(sent, 'item', 0, 0), axis=1)]
    another operation x6 -> x7, local copies, waits for them, and re-layouts: 3.9 us -> 6.71 us
  transfers between devices with their start and end apart: 3 -> 3, of which waited for: 3 -> 2; matrix products, arithmetic and copies ran while one was open for 3% -> 3% of each run, Pallas kernels for 0% -> 0%
where the time goes in v1:
time: 279 us; the launch traced here: 278 us
  waiting for transfers between devices  166 us (59%)
  other arithmetic  60.9 us (22%)
  matrix products  16 us (6%)
  between operations  14.9 us (5%)
  local copies, waits for them, and re-layouts  10.1 us (4%)
  starting transfers between devices  10.1 us (4%)
    psum x1, waiting for transfers between devices, body(): summed_rhs = lax.psum(local_rhs, 'band')  93 us
    all_gather x1, waiting for transfers between devices, body(): tags = lax.all_gather(tag_factors, 'item', axis=1, tiled=True)  72.7 us
    another operation x6, other arithmetic, finish_gram(): jnp.linalg.cholesky(summed_gram + REG * jnp.eye(rank, dtype=jnp.float32))  34.1 us
    another operation x3, other arithmetic, solve_rows(): lax.linalg.triangular_solve(factor, rhs, left_side=False, lower=True, tra...  19.7 us
    dot_general x4, matrix products, inner(): lax.dot_general(left, right, (((0,), (0,)), ((), ())), preferred_element_...  13.1 us
    all_to_all x1, starting transfers between devices, body(): users = jnp.concatenate(lax.all_to_all(sent, 'item', 0, 0), axis=1)  10.1 us
  transfers between devices with their start and end apart: 3, of which 2 were waited for; matrix products, arithmetic and copies ran while one was open for 3% of the time, Pallas kernels for 0%

profile of v1, /device:TPU:32, one launch (start us, length us, event | category | flops | bytes accessed | tf_op | source)
XLA Modules:
  0.0 278.4 jit_solution(17850497471540108323)
XLA Ops:
  6.5 2.9 %stack.2 = bf16[32,6144,8]{1,2,0:T(8,128)(2,1)} broadcast(bf16[6144,8]{0,1:T(8,128)(2,1)} %param.10), dimensions={1,2} | broadcast | bytes 3244032 | tf_op jit(solution)/shard_map/stack | solution.py:37
  9.4 10.1 %all-to-all-start = ((bf16[32,6144,8]{1,2,0:T(8,128)(2,1)}), bf16[32,6144,8]{1,2,0:T(8,128)(2,1)}, u32[]{:S(2)}, u32[]{:S(2)}) async-start(bf16[32,6144,8]{1,2,0:T(8,128)(2,1)} %stack.2), calls=%async_computation | async-start | bytes 6291456 | tf_op jit(solution)/shard_map/all_to_all | solution.py:38
  19.5 0.7 all-gather.2.cloned.1.call-update
  20.4 1.8 bitcast_multiply_fusion.1
  22.2 2.1 copy-done
  24.3 3.1 %bitcast_multiply_fusion = bf16[6144,512]{1,0:T(8,128)(2,1)} fusion(bf16[6144,512]{1,0:T(8,128)(2,1)S(1)} %copy-done, bf16[48,512]{1,0:T(8,128)(2,1)S(1)} %convert_element_type.7), kind=kLoop, calls=%fused_computation.2 | loop fusion | flops 3145728 | bytes 12632064 | tf_op jit(solution)/shard_map/mul | solution.py:13
  27.4 72.7 %all-gather.2.cloned.1.call-done = bf16[3072,256]{0,1:T(8,128)(2,1)} async-done(((bf16[3072,8]{0,1:T(8,128)(2,1)}), bf16[3072,256]{0,1:T(8,128)(2,1)}) %all-gather.2.cloned.1.call-update) | async-done | bytes 1572880 | tf_op jit(solution)/shard_map/all_gather | solution.py:39
  100.1 3.2 %convolution_multiply_fusion = f32[512,256]{1,0:T(8,128)} fusion(bf16[3072,512]{1,0:T(8,128)(2,1)S(1)} %copy-done.4, bf16[3072,256]{0,1:T(8,128)(2,1)} %all-gather.2.cloned.1.call-done), kind=kOutput, calls=%fused_computation.8 | convolution fusion | flops 805437440 | bytes 5242880 | tf_op jit(solution)/shard_map/dot_general | solution.py:18
  103.3 4.0 %fusion = f32[256,256]{1,0:T(8,128)S(1)} fusion(bf16[32,6144,8]{1,2,0:T(8,128)(2,1)} %all-to-all-done), kind=kOutput, calls=%fused_computation.3 | convolution fusion | flops 805306368 | bytes 3407872 | tf_op jit(solution)/shard_map/dot_general | solution.py:18
  107.4 1.3 fusion.7
  108.7 4.5 %fusion.4 = f32[512,256]{1,0:T(8,128)} fusion(f32[512,256]{1,0:T(8,128)S(1)} %copy-done.8, bf16[6144,512]{1,0:T(8,128)(2,1)S(1)} %copy-done.1, bf16[32,6144,8]{1,2,0:T(8,128)(2,1)} %all-to-all-done), kind=kOutput, calls=%fused_computation.9 | convolution fusion | flops 1610743808 | bytes 10485760 | tf_op jit(solution)/shard_map/dot_general | solution.py:18
  113.3 93.0 %all-reduce.4.cloned.1.call-done = (f32[512,256]{1,0:T(8,128)}, f32[256,256]{1,0:T(8,128)}) async-done(((f32[512,256]{1,0:T(8,128)}, f32[256,256]{1,0:T(8,128)}), (f32[512,256]{1,0:T(8,128)}, f32[256,256]{1,0:T(8,128)})) %all-reduce.4.cloned.1.call-update) | async-done | bytes 786448 | tf_op jit(solution)/shard_map/psum | solution.py:46
  206.3 1.0 select_add_fusion
  207.5 1.0 fusion.10
  208.5 11.7 %cholesky.49 = f32[128,128]{1,0:T(8,128)S(1)} custom-call(f32[128,128]{1,0:T(8,128)S(1)} %cholesky.115), custom_call_target="Cholesky" | custom-call | tf_op jit(solution)/shard_map/jit(cholesky)/cholesky | solution.py:33
  220.2 9.8 %custom-call.16 = f32[1,128,128]{1,2,0:T(8,128)S(1)} custom-call(f32[1,128,128]{2,1,0:T(8,128)S(1)} %get-tuple-element.28), custom_call_target="InvertDiagBlocksLowerTriangular" | custom-call | tf_op jit(solution)/shard_map/jit(cholesky)/cholesky | solution.py:33
  230.3 0.3 convolution_subtract_fusion.2
  230.6 11.9 %cholesky.103 = f32[128,128]{1,0:T(8,128)S(1)} custom-call(f32[128,128]{1,0:T(8,128)S(1)} %convolution_subtract_fusion.2), custom_call_target="Cholesky" | custom-call | tf_op jit(solution)/shard_map/jit(cholesky)/cholesky | solution.py:33
  242.5 0.7 compare_reduce_fusion
  244.5 3.8 %while.1 = (s32[]{:T(128)}, f32[256,256]{1,0:T(8,128)S(1)}, s32[2,2]{1,0:T(2,128)S(1)}, f32[2,128,128]{2,1,0:T(8,128)S(1)}, s32[]{:T(128)}) while((s32[]{:T(128)}, f32[256,256]{1,0:T(8,128)S(1)}, s32[2,2]{1,0:T(2,128)S(1)}, f32[2,128,128]{2,1,0:T(8,128)S(1)}, s32[]{:T(128)}) %tuple.23), condition=%wide.while_cond, body=%wide.while_body.sunk | while | flops 2 | bytes 131189 | solution.py:24
  244.5 0.6 fusion.33
  245.1 1.3 bitcast_dynamic-update-slice_fusion.2
  246.4 0.6 fusion.33
  247.0 1.3 bitcast_dynamic-update-slice_fusion.2
  248.3 19.7 %custom-call.17 = f32[2,128,128]{1,2,0:T(8,128)S(1)} custom-call(f32[2,128,128]{2,1,0:T(8,128)S(1)} %get-tuple-element.12), custom_call_target="InvertDiagBlocksLowerTriangular" | custom-call | tf_op jit(solution)/shard_map/triangular_solve | solution.py:24
  268.0 0.4 fusion.8
  268.4 0.4 convolution_subtract_fusion.1
  268.8 0.4 fusion.16
  269.1 0.4 fusion.15
  269.5 0.6 convolution_subtract_fusion
  270.1 0.4 fusion.14
  270.6 1.0 copy.11
  (36 shorter events, 0.8 us)
Async XLA Ops:
  9.4 10.9 %copy-start.7 = (s32[24,512]{1,0:T(8,128)S(1)}, s32[24,512]{1,0:T(8,128)}, u32[]{:S(2)}) copy-start(s32[24,512]{1,0:T(8,128)} %param.9) | copy-start | bytes 147460
  9.4 10.9 %copy-start.6 = (s32[48,512]{1,0:T(8,128)S(1)}, s32[48,512]{1,0:T(8,128)}, u32[]{:S(2)}) copy-start(s32[48,512]{1,0:T(8,128)} %param.7) | copy-start | bytes 294916
  9.4 10.9 %copy-start.3 = (bf16[3072,512]{1,0:T(8,128)(2,1)S(1)}, bf16[3072,512]{1,0:T(8,128)(2,1)}, u32[]{:S(2)}) copy-start(bf16[3072,512]{1,0:T(8,128)(2,1)} %param.8) | copy-start | bytes 9437188
  9.4 93.9 %all-to-all-start = ((bf16[32,6144,8]{1,2,0:T(8,128)(2,1)}), bf16[32,6144,8]{1,2,0:T(8,128)(2,1)}, u32[]{:S(2)}, u32[]{:S(2)}) async-start(bf16[32,6144,8]{1,2,0:T(8,128)(2,1)} %stack.2), calls=%async_computation | async-start | bytes 6291456 | tf_op jit(solution)/shard_map/all_to_all | solution.py:38
  19.5 80.6 %all-gather.2.cloned.1.call-start = ((), (), s32[]{:S(2)}) async-start(), calls=%async_computation.1 | async-start | bytes 1622016 | tf_op jit(solution)/shard_map/all_gather | solution.py:39
  20.2 186.1 %all-reduce.4.cloned.1.call-start = ((), (), s32[]{:S(2)}) async-start(), calls=%async_computation.2 | async-start | bytes 1572864 | tf_op jit(solution)/shard_map/psum | solution.py:46
  20.3 3.9 %copy-start = (bf16[6144,512]{1,0:T(8,128)(2,1)S(1)}, bf16[6144,512]{1,0:T(8,128)(2,1)}, u32[]{:S(2)}) copy-start(bf16[6144,512]{1,0:T(8,128)(2,1)} %param.6) | copy-start | bytes 18874372
  24.3 75.8 %copy-start.4 = (bf16[3072,512]{1,0:T(8,128)(2,1)S(1)}, bf16[3072,512]{1,0:T(8,128)(2,1)}, u32[]{:S(2)}) copy-start(bf16[3072,512]{1,0:T(8,128)(2,1)} %bitcast_multiply_fusion.1) | copy-start | bytes 9437188
  103.3 4.0 %copy-start.2 = (bf16[3072,256]{0,1:T(8,128)(2,1)S(1)}, bf16[3072,256]{0,1:T(8,128)(2,1)}, u32[]{:S(2)}) copy-start(bf16[3072,256]{0,1:T(8,128)(2,1)} %all-gather.2.cloned.1.call-done) | copy-start | bytes 4718596
  103.3 5.3 %copy-start.1 = (bf16[6144,512]{1,0:T(8,128)(2,1)S(1)}, bf16[6144,512]{1,0:T(8,128)(2,1)}, u32[]{:S(2)}) copy-start(bf16[6144,512]{1,0:T(8,128)(2,1)} %bitcast_multiply_fusion) | copy-start | bytes 18874372
  107.3 1.4 copy-start.8
  206.3 61.7 %copy-start.5 = (f32[512,256]{1,0:T(8,128)S(1)}, f32[512,256]{1,0:T(8,128)}, u32[]{:S(2)}) copy-start(f32[512,256]{1,0:T(8,128)} %get-tuple-element.21) | copy-start | bytes 1572868
Sparse Core Ops, SparseCore 0:
  22.2 77.8 all-gather.1
  113.4 92.8 all-reduce.3
